TPU v7x, 256 devices: a whole 4x4x8 slice. The times are simulated.
256 devices in a mesh: dp: 4 (over y), sx: 4 (over x_lo, core), sy: 16 (over z, x_hi).
Axes of the slice: x: 4 (x_hi: 2, x_lo: 2; x = x_hi * 2 + x_lo), y: 4, z: 8, core: 2. Of those that a mesh axis runs over, the one named last changes fastest.
Arguments:
- features: bfloat16 [4, 4, 16, 3072, 128], P('dp', 'sx', 'sy'), may hold values from -6 to 6
- cotangent: bfloat16 [4, 4, 16, 3072, 128], P('dp', 'sx', 'sy'), may hold values from -6 to 6
- weights: bfloat16 [27, 128, 128], replicated, may hold values from -0.109375 to 0.109375
- tables: int32 [4, 4, 16, 27, 24], P('dp', 'sx', 'sy'), may hold values from 0 to 56, as said below
- send_lists: int32 [4, 4, 16, 4], P('dp', 'sx', 'sy'), may hold values from 0 to 23, as said below
- counts: int32 [4, 4, 16], P('dp', 'sx', 'sy'), may hold values from 6 to 24, as said below
Outputs:
- output: bfloat16 [4, 4, 16, 3072, 128], P('dp', 'sx', 'sy')
- input_grad: bfloat16 [4, 4, 16, 3072, 128], P('dp', 'sx', 'sy')
- weight_grad: float32 [27, 128, 128], replicated
Inputs may be any that keep to these rules, and one draw needn't show every extreme that they name: `tables`: entries below 24 name a block of the tile, 24 + n * 4 + s' the s'-th sent block of neighbour direction n, 56 the empty block; under offset 27 // 2 every block reads itself. `send_lists`: the 4 blocks of one tile are distinct. `counts`: some tile has all 24 blocks active.
All inputs are finite; a program needn't handle non-finite values.
Results may differ from a plain program's by a relative error of at most 0.001.
Values may be sent and summed in bfloat16 or wider, within the bound.
A program may use at most 64 MiB of HBM per device.

v0:
```python
import math

import jax
import jax.numpy as jnp
from jax import lax
from jax.sharding import PartitionSpec as P

directions = ((-1, -1), (-1, 0), (-1, 1), (0, -1), (0, 1), (1, -1), (1, 0), (1, 1))


def shifted(block, axis, distance):
    devices = range(lax.axis_size(axis))
    route = [(i - distance, i) for i in devices if i - distance in devices]
    return lax.ppermute(block, axis, route)


def padded(cells, sides, width):
    for axis, dim in sides:
        count = lax.axis_size(axis)
        ends = count - 1
        head = lax.slice_in_dim(cells, 0, width, axis=dim)
        tail = lax.slice_in_dim(cells, cells.shape[dim] - width, cells.shape[dim], axis=dim)
        cells = jnp.concatenate(
            [
                lax.ppermute(tail, axis, [(i, (i + 1) % count) for i in range(ends)]),
                cells,
                lax.ppermute(head, axis, [((i + 1) % count, i) for i in range(ends)]),
            ],
            axis=dim,
        )
    return cells


def local(features, cotangent, weights, tables, send_lists, counts):
    num_blocks = tables.shape[4]
    num_sent = send_lists.shape[3]
    offsets = weights.shape[0]
    channels = weights.shape[1]
    width_block = features.shape[3] // num_blocks
    group_size = 4
    active = (jnp.arange(num_blocks) < counts.reshape(())).astype(jnp.bfloat16)[:, None, None]
    active_full = active.astype(jnp.float32)
    blocks_in = features.reshape(num_blocks, width_block, channels) * active
    blocks_grad = cotangent.reshape(num_blocks, width_block, channels) * active
    offset_table = tables.reshape(offsets, num_blocks)
    sent_ids = send_lists.reshape(num_sent)
    groups = jnp.arange(num_blocks // group_size)

    def grad_group(accum, group):
        start = group * group_size
        picks = lax.dynamic_slice_in_dim(offset_table, start, group_size, 1)
        grad_rows = lax.dynamic_slice_in_dim(blocks_grad, start, group_size, 0)
        contrib = jnp.einsum(
            "gvd,kcd->kgvc", grad_rows, weights, preferred_element_type=jnp.float32
        )
        accum = accum.at[picks.reshape(-1)].add(
            contrib.reshape(offsets * group_size, width_block, channels)
        )
        return (accum, None)

    num_ext = num_blocks + 8 * num_sent + 1
    grad_ext, unused_rows = lax.scan(
        grad_group, jnp.zeros((num_ext, width_block, channels), jnp.float32), groups
    )
    halo_grads = grad_ext[num_blocks : num_blocks + 8 * num_sent].reshape(
        8, num_sent * width_block, channels
    )
    received = jnp.zeros((num_sent * width_block, channels), jnp.float32)
    for slot_index, (step_x, step_y) in enumerate(directions):
        portion = halo_grads[slot_index]
        if step_x != 0:
            portion = shifted(portion, "sx", step_x)
        if step_y != 0:
            portion = shifted(portion, "sy", step_y)
        received = received + portion
    local_grad = (
        grad_ext[:num_blocks].at[sent_ids].add(received.reshape(num_sent, width_block, channels))
    )
    input_grad = (local_grad * active_full).astype(jnp.bfloat16).reshape(features.shape)
    outgoing = blocks_in[sent_ids].reshape(1, 1, num_sent * width_block, channels)
    bordered = padded(outgoing, (("sx", 0), ("sy", 1)), 1)
    neighbours = [
        bordered[1 + step_x, 1 + step_y].reshape(num_sent, width_block, channels)
        for step_x, step_y in directions
    ]
    extended = jnp.concatenate(
        [blocks_in] + neighbours + [jnp.zeros((1, width_block, channels), jnp.bfloat16)], axis=0
    )

    def forward_group(accum, group):
        start = group * group_size
        picks = lax.dynamic_slice_in_dim(offset_table, start, group_size, 1)
        gathered = extended[picks]
        grad_rows = lax.dynamic_slice_in_dim(blocks_grad, start, group_size, 0)
        rows_active = lax.dynamic_slice_in_dim(active_full, start, group_size, 0)
        outputs = jnp.einsum("kgvc,kcd->gvd", gathered, weights, preferred_element_type=jnp.float32)
        accum = accum + jnp.einsum(
            "kgvc,gvd->kcd", gathered, grad_rows, preferred_element_type=jnp.float32
        )
        return (accum, (outputs * rows_active).astype(jnp.bfloat16))

    weight_part, outputs = lax.scan(
        forward_group, jnp.zeros((offsets, channels, channels), jnp.float32), groups
    )
    output = outputs.reshape(features.shape)
    total = (
        num_blocks * width_block * lax.axis_size("dp") * lax.axis_size("sx") * lax.axis_size("sy")
    )
    scaled_part = weight_part * (1.0 / math.sqrt(total))
    weight_grad = lax.psum(scaled_part, ("dp", "sx", "sy"))
    return (output, input_grad, weight_grad)


def solution(mesh):
    return jax.shard_map(
        local,
        mesh=mesh,
        in_specs=(
            P("dp", "sx", "sy", None, None),
            P("dp", "sx", "sy", None, None),
            P(),
            P("dp", "sx", "sy", None, None),
            P("dp", "sx", "sy", None),
            P("dp", "sx", "sy"),
        ),
        out_specs=(P("dp", "sx", "sy", None, None), P("dp", "sx", "sy", None, None), P()),
        check_vma=False,
    )
```

profile of v0, /device:TPU:1, one launch (start us, length us, event | category | flops | bytes accessed | tf_op | source)
XLA Modules:
  0.0 616.3 jit_solution(9292657915912878841)
XLA Ops:
  8.5 3.2 constant_dynamic-update-slice_fusion.9
  12.3 5.1 collective-permute-start.1
  22.5 184.1 %while.23 = (s32[]{:T(128)}, f32[57,128,128]{2,1,0:T(8,128)}, s32[6]{0:T(128)S(1)}, s32[27,24]{1,0:T(8,128)}, bf16[24,128,128]{2,1,0:T(8,128)(2,1)}, /*index=5*/...) while((s32[]{:T(128)}, f32[57,128,128]{2,1,0:T(8,128)}, s32[6]{0:T(128)S(1)}, ...), condition=%wide.region_4.5_spmd, body=%wide.region_2.0_spmd.sunk | while | flops 454754624 | bytes 43486336 | solution.py:62
  27.0 3.3 copy.22
  30.3 22.8 %scatter_fusion = f32[57,128,128]{2,1,0:T(8,128)} fusion(f32[57,128,128]{2,1,0:T(8,128)} %get-tuple-element.307, s32[108]{0:T(128)S(1)} %fusion.33, f32[108,128,128]{2,1,0:T(8,128)} %bitcast.107), kind=kCustom, calls=%fused_computation.2.clone.1 | custom fusion | flops 1769472 | bytes 21234096 | tf_op jit(solution)/shard_map/while/body/eval_jaxpr/scatter-add | solution.py:56
  57.7 3.3 copy.22
  61.0 22.9 %scatter_fusion = f32[57,128,128]{2,1,0:T(8,128)} fusion(f32[57,128,128]{2,1,0:T(8,128)} %get-tuple-element.307, s32[108]{0:T(128)S(1)} %fusion.33, f32[108,128,128]{2,1,0:T(8,128)} %bitcast.107), kind=kCustom, calls=%fused_computation.2.clone.1 | custom fusion | flops 1769472 | bytes 21234096 | tf_op jit(solution)/shard_map/while/body/eval_jaxpr/scatter-add | solution.py:56
  88.4 3.3 copy.22
  91.7 22.8 %scatter_fusion = f32[57,128,128]{2,1,0:T(8,128)} fusion(f32[57,128,128]{2,1,0:T(8,128)} %get-tuple-element.307, s32[108]{0:T(128)S(1)} %fusion.33, f32[108,128,128]{2,1,0:T(8,128)} %bitcast.107), kind=kCustom, calls=%fused_computation.2.clone.1 | custom fusion | flops 1769472 | bytes 21234096 | tf_op jit(solution)/shard_map/while/body/eval_jaxpr/scatter-add | solution.py:56
  119.0 3.3 copy.22
  122.3 22.9 %scatter_fusion = f32[57,128,128]{2,1,0:T(8,128)} fusion(f32[57,128,128]{2,1,0:T(8,128)} %get-tuple-element.307, s32[108]{0:T(128)S(1)} %fusion.33, f32[108,128,128]{2,1,0:T(8,128)} %bitcast.107), kind=kCustom, calls=%fused_computation.2.clone.1 | custom fusion | flops 1769472 | bytes 21234096 | tf_op jit(solution)/shard_map/while/body/eval_jaxpr/scatter-add | solution.py:56
  149.8 3.3 copy.22
  153.1 22.9 %scatter_fusion = f32[57,128,128]{2,1,0:T(8,128)} fusion(f32[57,128,128]{2,1,0:T(8,128)} %get-tuple-element.307, s32[108]{0:T(128)S(1)} %fusion.33, f32[108,128,128]{2,1,0:T(8,128)} %bitcast.107), kind=kCustom, calls=%fused_computation.2.clone.1 | custom fusion | flops 1769472 | bytes 21234096 | tf_op jit(solution)/shard_map/while/body/eval_jaxpr/scatter-add | solution.py:56
  180.5 3.3 copy.22
  183.8 22.9 %scatter_fusion = f32[57,128,128]{2,1,0:T(8,128)} fusion(f32[57,128,128]{2,1,0:T(8,128)} %get-tuple-element.307, s32[108]{0:T(128)S(1)} %fusion.33, f32[108,128,128]{2,1,0:T(8,128)} %bitcast.107), kind=kCustom, calls=%fused_computation.2.clone.1 | custom fusion | flops 1769472 | bytes 21234096 | tf_op jit(solution)/shard_map/while/body/eval_jaxpr/scatter-add | solution.py:56
  206.7 4.6 collective-permute-start.2
  216.1 3.1 collective-permute-start.6
  226.3 13.2 %collective-permute-done.3 = bf16[3,1,512,128]{3,2,1,0:T(8,128)(2,1)S(1)} collective-permute-done((bf16[3,1,512,128]{3,2,1,0:T(8,128)(2,1)S(1)}, bf16[3,1,512,128]{3,2,1,0:T(8,128)(2,1)S(1)}, u32[]{:S(2)}, u32[]{:S(2)}) %collective-permute-start.3) | collective-permute-done | bytes 393248 | tf_op jit(solution)/shard_map/ppermute | solution.py:27
  239.5 3.0 collective-permute-start.10
  247.7 79.9 %while.24 = (s32[]{:T(128)}, f32[27,128,128]{2,1,0:T(8,128)}, bf16[6,4,128,128]{3,2,1,0:T(8,128)(2,1)}, s32[6]{0:T(128)}, s32[27,24]{1,0:T(8,128)}, /*index=5*/b...) while((s32[]{:T(128)}, f32[27,128,128]{2,1,0:T(8,128)}, ...), condition=%wide.region_1.0_spmd.clone, body=%wide.region_0.1_spmd.clone.sunk | while | flops 906986816 | bytes 33004880 | solution.py:102
  253.9 3.0 fusion.39
  267.2 3.0 fusion.39
  280.5 3.0 fusion.39
  293.8 3.0 fusion.39
  307.1 3.0 fusion.39
  320.4 3.0 fusion.39
  327.6 4.3 collective-permute-start.7
  338.1 5.5 collective-permute-start.15
  345.0 5.5 collective-permute-start.8
  353.3 11.4 %collective-permute-done.15 = f32[512,128]{1,0:T(8,128)S(1)} collective-permute-done((f32[512,128]{1,0:T(8,128)}, f32[512,128]{1,0:T(8,128)S(1)}, u32[]{:S(2)}, u32[]{:S(2)}) %collective-permute-start.15) | collective-permute-done | bytes 262176 | tf_op jit(solution)/shard_map/ppermute | solution.py:14
  364.8 5.8 collective-permute-done.8
  373.6 232.9 %all-reduce.2.cloned.1.call-done = f32[27,128,128]{2,1,0:T(8,128)} async-done(((f32[27,128,128]{2,1,0:T(8,128)}), f32[27,128,128]{2,1,0:T(8,128)}) %all-reduce.2.cloned.1.call-update) | async-done | bytes 1769488 | tf_op jit(solution)/shard_map/psum | solution.py:110
  (154 shorter events, 120.1 us)
Async XLA Ops:
  7.2 599.4 %all-reduce.2.cloned.1.call-start = ((), (), s32[]{:S(2)}) async-start(), calls=%async_computation | async-start | bytes 3538944 | tf_op jit(solution)/shard_map/psum | solution.py:110
  8.5 10.9 %copy-start.3 = (s32[1,1,1,27,24]{3,4,2,1,0:T(8,128)S(1)}, s32[1,1,1,27,24]{3,4,2,1,0:T(8,128)}, u32[]{:S(2)}) copy-start(s32[1,1,1,27,24]{3,4,2,1,0:T(8,128)} %param.13) | copy-start | bytes 7780
  12.3 194.3 %collective-permute-start.1 = (bf16[1,1,512,128]{3,2,1,0:T(8,128)(2,1)S(1)}, bf16[1,1,512,128]{3,2,1,0:T(8,128)(2,1)S(1)}, u32[]{:S(2)}, u32[]{:S(2)}) collective-permute-start(bf16[1,1,512,128]{3,2,1,0:T(8,128)(2,1)S(1)} %bitcast.116), channel_id=1, source_target_pairs={{16,0},{32,16},{48,32},{17,1},{33,17},{49,33},{18,2},{34,18},{50,3... | collective-permute-start | bytes 393224 | tf_op jit(solution)/shard_map/ppermute | solution.py:27
  17.5 189.2 %collective-permute-start = (bf16[1,1,512,128]{3,2,1,0:T(8,128)(2,1)S(1)}, bf16[1,1,512,128]{3,2,1,0:T(8,128)(2,1)S(1)}, u32[]{:S(2)}, u32[]{:S(2)}) collective-permute-start(bf16[1,1,512,128]{3,2,1,0:T(8,128)(2,1)S(1)} %bitcast.117), channel_id=1, source_target_pairs={{0,16},{16,32},{32,48},{1,17},{17,33},{33,49},{2,18},{18,34},{34,5... | collective-permute-start | bytes 393224 | tf_op jit(solution)/shard_map/ppermute | solution.py:25
  206.7 17.0 %collective-permute-start.2 = (bf16[3,1,512,128]{3,2,1,0:T(8,128)(2,1)S(1)}, bf16[3,1,512,128]{3,2,1,0:T(8,128)(2,1)S(1)}, u32[]{:S(2)}, u32[]{:S(2)}) collective-permute-start(bf16[3,1,512,128]{3,2,1,0:T(8,128)(2,1)S(1)} %pad_maximum_fusion), channel_id=1, source_target_pairs={{0,1},{1,2},{2,3},{3,4},{4,5},{5,6},{6,7},{7,8},{8,9},{9,10},{10,1... | collective-permute-start | bytes 1179656 | tf_op jit(solution)/shard_map/ppermute | solution.py:25
  214.2 113.4 %collective-permute-start.14 = (f32[512,128]{1,0:T(8,128)}, f32[512,128]{1,0:T(8,128)}, u32[]{:S(2)}, u32[]{:S(2)}) collective-permute-start(f32[512,128]{1,0:T(8,128)} %bitcast.30), channel_id=1, source_target_pairs={{0,16},{16,32},{32,48},{1,17},{17,33},{33,49},{2,18},{18,34},{34,5... | collective-permute-start | bytes 786440 | tf_op jit(solution)/shard_map/ppermute | solution.py:14
  216.1 115.7 %collective-permute-start.6 = (f32[512,128]{1,0:T(8,128)}, f32[512,128]{1,0:T(8,128)}, u32[]{:S(2)}, u32[]{:S(2)}) collective-permute-start(f32[512,128]{1,0:T(8,128)} %bitcast.24), channel_id=1, source_target_pairs={{16,0},{32,16},{48,32},{17,1},{33,17},{49,33},{18,2},{34,18},{50,3... | collective-permute-start | bytes 786440 | tf_op jit(solution)/shard_map/ppermute | solution.py:14
  219.3 117.5 %collective-permute-start.13 = (f32[512,128]{1,0:T(8,128)}, f32[512,128]{1,0:T(8,128)}, u32[]{:S(2)}, u32[]{:S(2)}) collective-permute-start(f32[512,128]{1,0:T(8,128)} %bitcast.29), channel_id=1, source_target_pairs={{0,16},{16,32},{32,48},{1,17},{17,33},{33,49},{2,18},{18,34},{34,5... | collective-permute-start | bytes 786440 | tf_op jit(solution)/shard_map/ppermute | solution.py:14
  221.7 116.4 %collective-permute-start.11 = (f32[512,128]{1,0:T(8,128)}, f32[512,128]{1,0:T(8,128)}, u32[]{:S(2)}, u32[]{:S(2)}) collective-permute-start(f32[512,128]{1,0:T(8,128)} %bitcast.28), channel_id=1, source_target_pairs={{0,16},{16,32},{32,48},{1,17},{17,33},{33,49},{2,18},{18,34},{34,5... | collective-permute-start | bytes 786440 | tf_op jit(solution)/shard_map/ppermute | solution.py:14
  223.7 15.8 %collective-permute-start.3 = (bf16[3,1,512,128]{3,2,1,0:T(8,128)(2,1)S(1)}, bf16[3,1,512,128]{3,2,1,0:T(8,128)(2,1)S(1)}, u32[]{:S(2)}, u32[]{:S(2)}) collective-permute-start(bf16[3,1,512,128]{3,2,1,0:T(8,128)(2,1)S(1)} %pad_maximum_fusion), channel_id=1, source_target_pairs={{1,0},{2,1},{3,2},{4,3},{5,4},{6,5},{7,6},{8,7},{9,8},{10,9},{11,1... | collective-permute-start | bytes 1179656 | tf_op jit(solution)/shard_map/ppermute | solution.py:27
  239.5 104.2 %collective-permute-start.10 = (f32[512,128]{1,0:T(8,128)}, f32[512,128]{1,0:T(8,128)}, u32[]{:S(2)}, u32[]{:S(2)}) collective-permute-start(f32[512,128]{1,0:T(8,128)} %bitcast.27), channel_id=1, source_target_pairs={{0,1},{1,2},{2,3},{3,4},{4,5},{5,6},{6,7},{7,8},{8,9},{9,10},{10,1... | collective-permute-start | bytes 786440 | tf_op jit(solution)/shard_map/ppermute | solution.py:14
  253.8 3.1 copy-start
  259.8 1.2 copy-start.1
  267.2 3.1 copy-start
  273.1 1.2 copy-start.1
  280.5 3.1 copy-start
  286.4 1.2 copy-start.1
  293.8 3.1 copy-start
  299.7 1.2 copy-start.1
  307.1 3.1 copy-start
  313.1 1.2 copy-start.1
  320.4 3.1 copy-start
  326.4 1.2 copy-start.1
  327.6 17.4 %collective-permute-start.7 = (f32[512,128]{1,0:T(8,128)}, f32[512,128]{1,0:T(8,128)S(1)}, u32[]{:S(2)}, u32[]{:S(2)}) collective-permute-start(f32[512,128]{1,0:T(8,128)} %bitcast.127), channel_id=1, source_target_pairs={{16,0},{32,16},{48,32},{17,1},{33,17},{49,33},{18,2},{34,18},{50,3... | collective-permute-start | bytes 786440 | tf_op jit(solution)/shard_map/ppermute | solution.py:14
  331.9 18.6 %collective-permute-start.4 = (f32[512,128]{1,0:T(8,128)}, f32[512,128]{1,0:T(8,128)S(1)}, u32[]{:S(2)}, u32[]{:S(2)}) collective-permute-start(f32[512,128]{1,0:T(8,128)} %bitcast.126), channel_id=1, source_target_pairs={{16,0},{32,16},{48,32},{17,1},{33,17},{49,33},{18,2},{34,18},{50,3... | collective-permute-start | bytes 786440 | tf_op jit(solution)/shard_map/ppermute | solution.py:14
  333.8 3.0 copy-start.2
  336.8 16.5 %collective-permute-start.9 = (f32[512,128]{1,0:T(8,128)S(1)}, f32[512,128]{1,0:T(8,128)S(1)}, u32[]{:S(2)}, u32[]{:S(2)}) collective-permute-start(f32[512,128]{1,0:T(8,128)S(1)} %bitcast.125), channel_id=1, source_target_pairs={{1,0},{2,1},{3,2},{4,3},{5,4},{6,5},{7,6},{8,7},{9,8},{10,9},{11,1... | collective-permute-start | bytes 786440 | tf_op jit(solution)/shard_map/ppermute | solution.py:14
  338.1 26.6 %collective-permute-start.15 = (f32[512,128]{1,0:T(8,128)}, f32[512,128]{1,0:T(8,128)S(1)}, u32[]{:S(2)}, u32[]{:S(2)}) collective-permute-start(f32[512,128]{1,0:T(8,128)} %collective-permute-done.14), channel_id=1, source_target_pairs={{0,1},{1,2},{2,3},{3,4},{4,5},{5,6},{6,7},{7,8},{8,9},{9,10},{10,1... | collective-permute-start | bytes 786440 | tf_op jit(solution)/shard_map/ppermute | solution.py:14
  343.7 21.1 %collective-permute-start.12 = (f32[512,128]{1,0:T(8,128)}, f32[512,128]{1,0:T(8,128)S(1)}, u32[]{:S(2)}, u32[]{:S(2)}) collective-permute-start(f32[512,128]{1,0:T(8,128)} %collective-permute-done.11), channel_id=1, source_target_pairs={{1,0},{2,1},{3,2},{4,3},{5,4},{6,5},{7,6},{8,7},{9,8},{10,9},{11,1... | collective-permute-start | bytes 786440 | tf_op jit(solution)/shard_map/ppermute | solution.py:14
  345.0 25.6 %collective-permute-start.8 = (f32[512,128]{1,0:T(8,128)S(1)}, f32[512,128]{1,0:T(8,128)S(1)}, u32[]{:S(2)}, u32[]{:S(2)}) collective-permute-start(f32[512,128]{1,0:T(8,128)S(1)} %collective-permute-done.7), channel_id=1, source_target_pairs={{0,1},{1,2},{2,3},{3,4},{4,5},{5,6},{6,7},{7,8},{8,9},{9,10},{10,1... | collective-permute-start | bytes 786440 | tf_op jit(solution)/shard_map/ppermute | solution.py:14
  350.5 20.1 %collective-permute-start.5 = (f32[512,128]{1,0:T(8,128)S(1)}, f32[512,128]{1,0:T(8,128)S(1)}, u32[]{:S(2)}, u32[]{:S(2)}) collective-permute-start(f32[512,128]{1,0:T(8,128)S(1)} %collective-permute-done.4), channel_id=1, source_target_pairs={{1,0},{2,1},{3,2},{4,3},{5,4},{6,5},{7,6},{8,7},{9,8},{10,9},{11,1... | collective-permute-start | bytes 786440 | tf_op jit(solution)/shard_map/ppermute | solution.py:14
Sparse Core Ops, SparseCore 0:
  336.9 269.6 all-reduce.1
where the time goes:
time: 621 us; the launch traced here: 616 us
  waiting for transfers between devices  263 us (42%)
  other arithmetic  152 us (24%)
  local copies, waits for them, and re-layouts  81.9 us (13%)
  matrix products  49.6 us (8%)
  starting transfers between devices  46.6 us (8%)
  between operations  15 us (2%)
  loops' own time  7.98 us (1%)
    psum x1, waiting for transfers between devices, local(): weight_grad = lax.psum(scaled_part, ('dp', 'sx', 'sy'))  233 us
    scatter-add x6, other arithmetic, grad_group(): accum.at[picks.reshape(-1)]  137 us
    ppermute x12, starting transfers between devices, shifted(): return lax.ppermute(block, axis, route)  33.5 us
    transpose x6, local copies, waits for them, and re-layouts, grad_group(): jnp.einsum('gvd,kcd->kgvc', grad_rows, weights, preferred_element_type=jn...  20.1 us
    dot_general x6, matrix products, forward_group(): jnp.einsum('kgvc,kcd->gvd', gathered, weights, preferred_element_type=jnp...  18.2 us
    dot_general x6, matrix products, forward_group(): jnp.einsum('kgvc,gvd->kcd', gathered, grad_rows, preferred_element_type=j...  17.3 us
    ppermute x12, waiting for transfers between devices, shifted(): return lax.ppermute(block, axis, route)  17.3 us
    gather x6, local copies, waits for them, and re-layouts, forward_group(): gathered = extended[picks]  16.4 us
  transfers between devices with their start and end apart: 17, of which 4 were waited for; matrix products, arithmetic and copies ran while one was open for 44% of the time, Pallas kernels for 0%

commit v1 on v0

v1 whole, which is shorter than its diff:
```python
import functools
import math

import jax
import jax.numpy as jnp
from jax import lax
from jax.experimental import pallas as pl
from jax.experimental.pallas import tpu as pltpu
from jax.sharding import PartitionSpec as P

MESH = pl.DeviceIdType.MESH
F32 = jnp.float32
BF16 = jnp.bfloat16


def scatter_body(tables, sends, counts, feats, cot, weights, outgoing, grad_ext, grads, turned):
    num_blocks, rows, channels = cot.shape
    offsets = weights.shape[0]
    pairs = offsets // 2
    group = 4 if num_blocks % 4 == 0 else num_blocks
    count = counts[0, 0]

    grad_ext[...] = jnp.zeros_like(grad_ext)
    for s in range(outgoing.shape[0]):
        block = sends[0, s]
        outgoing[s] = jnp.where(block < count, feats[block], jnp.zeros((rows, channels), BF16))
    for b in range(num_blocks):
        grads[b] = jnp.where(b < count, cot[b], jnp.zeros((rows, channels), BF16))

    def turn(k, carry):
        turned[k] = weights[k].T
        return carry

    lax.fori_loop(0, offsets, turn, 0)

    def pair(p, carry):
        both = jnp.concatenate([turned[2 * p], turned[2 * p + 1]], axis=1)
        for first in range(0, num_blocks, group):
            lhs = grads[first : first + group].reshape(group * rows, channels)
            terms = jnp.dot(lhs, both, preferred_element_type=F32)
            for i in range(group):
                term = terms[i * rows : (i + 1) * rows]
                grad_ext[tables[first + i, 2 * p]] += term[:, :channels]
                grad_ext[tables[first + i, 2 * p + 1]] += term[:, channels:]
        return carry

    lax.fori_loop(0, pairs, pair, 0)
    for k in range(2 * pairs, offsets):
        for first in range(0, num_blocks, group):
            lhs = grads[first : first + group].reshape(group * rows, channels)
            terms = jnp.dot(lhs, turned[k], preferred_element_type=F32)
            for i in range(group):
                grad_ext[tables[first + i, k]] += terms[i * rows : (i + 1) * rows]


def main_body(
    sizes,
    tables,
    sends,
    counts,
    feats,
    cot,
    weights,
    outgoing,
    grad_ext,
    out_hbm,
    grad_hbm,
    weight_hbm,
    ext,
    turned,
    grads,
    taps,
    own_grad,
    from_x,
    to_y,
    from_y,
    returned,
    part,
    from_core,
    from_plane,
    plane_sum,
    from_z,
    plane_full,
    full,
    total,
    out_block,
    grad_block,
    in_sem,
    out_sem,
    fy_send,
    fy_recv,
    fx_send,
    fx_recv,
    bx_send,
    bx_recv,
    by_send,
    by_recv,
    c_send,
    c_recv,
    p_send,
    p_recv,
    z_send,
    z_recv,
    gz_send,
    gz_recv,
    gp_send,
    gp_recv,
    gc_send,
    gc_recv,
):
    n_y, n_sx, n_sy = sizes
    n_lo, n_hi, n_z = n_sx // 2, 2, n_sy // 2
    n_x = n_lo * n_hi
    n_plane = n_x * n_y
    num_blocks, rows, channels = cot.shape
    offsets = weights.shape[0]
    num_sent = outgoing.shape[0]
    half = part.shape[0] // 2
    piece = channels // n_plane
    z_depth = from_z.shape[1]
    count = counts[0, 0]

    y, sx, sy = lax.axis_index("dp"), lax.axis_index("sx"), lax.axis_index("sy")
    core, lo, hi, z = lax.rem(sx, 2), sx // 2, lax.rem(sy, 2), sy // 2
    here = y * n_x + hi * n_lo + lo

    def device(dp, x, t):
        return {"dp": dp, "sx": x, "sy": t}

    def plane_device(p):
        py, px = p // n_x, lax.rem(p, n_x)
        return device(py, lax.rem(px, n_lo) * 2 + core, z * 2 + px // n_lo)

    def z_device(level):
        return device(y, sx, level * 2 + hi)

    partner = device(y, sx + 1 - 2 * core, sy)
    west, east = device(y, sx - 1, sy), device(y, sx + 1, sy)
    south, north = device(y, sx, sy - 1), device(y, sx, sy + 1)
    has_west, has_east = sx > 0, sx < n_sx - 1
    has_south, has_north = sy > 0, sy < n_sy - 1

    barrier = pltpu.get_barrier_semaphore()
    for there, target in (
        (has_west, west),
        (has_east, east),
        (has_south, south),
        (has_north, north),
    ):

        @pl.when(there)
        def _():
            pl.semaphore_signal(barrier, inc=1, device_id=target, device_id_type=MESH)

    pl.semaphore_signal(barrier, inc=1, device_id=partner, device_id_type=MESH)

    def greet_plane(d, carry):
        target = plane_device(lax.rem(here + d, n_plane))
        pl.semaphore_signal(barrier, inc=1, device_id=target, device_id_type=MESH)
        return carry

    def greet_z(d, carry):
        target = z_device(lax.rem(z + d, n_z))
        pl.semaphore_signal(barrier, inc=1, device_id=target, device_id_type=MESH)
        return carry

    lax.fori_loop(1, n_plane, greet_plane, 0)
    lax.fori_loop(1, n_z, greet_z, 0)

    loads = [
        pltpu.make_async_copy(feats, ext.at[pl.ds(0, num_blocks)], in_sem.at[0]),
        pltpu.make_async_copy(cot, grads, in_sem.at[1]),
        pltpu.make_async_copy(weights, taps.at[pl.ds(0, offsets)], in_sem.at[2]),
        pltpu.make_async_copy(grad_ext.at[pl.ds(0, num_blocks)], own_grad, in_sem.at[3]),
    ]
    for load in loads:
        load.start()

    greeters = n_plane + n_z - 1
    greeters = greeters + jnp.where(has_west, 1, 0) + jnp.where(has_east, 1, 0)
    greeters = greeters + jnp.where(has_south, 1, 0) + jnp.where(has_north, 1, 0)
    pl.semaphore_wait(barrier, greeters)

    def remote(src, dst, send, recv, target):
        return pltpu.make_async_remote_copy(
            src_ref=src,
            dst_ref=dst,
            send_sem=send,
            recv_sem=recv,
            device_id=target,
            device_id_type=MESH,
        )

    base = num_blocks

    def slots(n):
        return ext.at[pl.ds(base + n * num_sent, num_sent)]

    to_north = remote(outgoing, slots(3), fy_send.at[0], fy_recv.at[0], north)
    to_south = remote(outgoing, slots(4), fy_send.at[1], fy_recv.at[1], south)
    to_east = [
        remote(outgoing, slots(1), fx_send.at[0], fx_recv.at[0], east),
        remote(slots(3), slots(0), fx_send.at[1], fx_recv.at[1], east),
        remote(slots(4), slots(2), fx_send.at[2], fx_recv.at[2], east),
    ]
    to_west = [
        remote(outgoing, slots(6), fx_send.at[3], fx_recv.at[3], west),
        remote(slots(3), slots(5), fx_send.at[4], fx_recv.at[4], west),
        remote(slots(4), slots(7), fx_send.at[5], fx_recv.at[5], west),
    ]
    grads_west = remote(
        grad_ext.at[pl.ds(base, 3 * num_sent)], from_x.at[1], bx_send.at[0], bx_recv.at[0], west
    )
    grads_east = remote(
        grad_ext.at[pl.ds(base + 5 * num_sent, 3 * num_sent)],
        from_x.at[0],
        bx_send.at[1],
        bx_recv.at[1],
        east,
    )

    @pl.when(has_north)
    def _():
        to_north.start()

    @pl.when(has_south)
    def _():
        to_south.start()

    @pl.when(has_east)
    def _():
        to_east[0].start()

    @pl.when(has_west)
    def _():
        to_west[0].start()

    zeros = jnp.zeros((rows, channels), BF16)
    sent_zeros = jnp.zeros((num_sent, rows, channels), BF16)

    def clear(n):
        ext[base + n * num_sent : base + (n + 1) * num_sent] = sent_zeros

    @pl.when(jnp.logical_not(has_south))
    def _():
        clear(3)
        clear(0)
        clear(5)

    @pl.when(jnp.logical_not(has_north))
    def _():
        clear(4)
        clear(2)
        clear(7)

    @pl.when(jnp.logical_not(has_west))
    def _():
        clear(1)

        @pl.when(has_south)
        def _():
            clear(0)

        @pl.when(has_north)
        def _():
            clear(2)

    @pl.when(jnp.logical_not(has_east))
    def _():
        clear(6)

        @pl.when(has_south)
        def _():
            clear(5)

        @pl.when(has_north)
        def _():
            clear(7)

    empty = base + 8 * num_sent
    ext[empty] = zeros
    turned[empty] = zeros
    taps[offsets] = jnp.zeros((channels, channels), BF16)
    returned[num_sent] = jnp.zeros((rows, channels), F32)

    loads[0].wait()
    for b in range(num_blocks):
        block = jnp.where(b < count, ext[b], zeros)
        ext[b] = block
        turned[b] = block.T
    loads[1].wait()
    for b in range(num_blocks):
        grads[b] = jnp.where(b < count, grads[b], zeros)

    @pl.when(has_south)
    def _():
        to_north.wait_recv()

        @pl.when(has_east)
        def _():
            to_east[1].start()

        @pl.when(has_west)
        def _():
            to_west[1].start()

    @pl.when(has_north)
    def _():
        to_south.wait_recv()

        @pl.when(has_east)
        def _():
            to_east[2].start()

        @pl.when(has_west)
        def _():
            to_west[2].start()

    @pl.when(has_east)
    def _():
        grads_east.start()

    @pl.when(has_west)
    def _():
        grads_west.start()

    def turn(n):
        for s in range(num_sent):
            turned[base + n * num_sent + s] = ext[base + n * num_sent + s].T

    turn(3)
    turn(4)

    @pl.when(has_west)
    def _():
        to_east[0].wait_recv()

        @pl.when(has_south)
        def _():
            to_east[1].wait_recv()

        @pl.when(has_north)
        def _():
            to_east[2].wait_recv()

    @pl.when(has_east)
    def _():
        to_west[0].wait_recv()

        @pl.when(has_south)
        def _():
            to_west[1].wait_recv()

        @pl.when(has_north)
        def _():
            to_west[2].wait_recv()

    for n in (0, 1, 2, 5, 6, 7):
        turn(n)

    chunk = half // 2

    def weight_terms(first):
        def step(pair, carry):
            rhs = grads[pl.ds(2 * pair, 2)].reshape(2 * rows, channels)
            parts = []
            for i in range(chunk):
                k = jnp.minimum(first + i, offsets - 1)
                parts.append(
                    jnp.concatenate(
                        [turned[tables[2 * pair, k]], turned[tables[2 * pair + 1, k]]], axis=1
                    )
                )
            lhs = jnp.concatenate(parts, axis=0)
            terms = jnp.dot(lhs, rhs, preferred_element_type=F32)
            part[pl.ds(first, chunk)] += terms.reshape(chunk, channels, channels)
            return carry

        part[pl.ds(first, chunk)] = jnp.zeros((chunk, channels, channels), F32)
        lax.fori_loop(0, num_blocks // 2, step, 0)

    own, other = core * half, (1 - core) * half
    to_core = []
    for c in range(2):
        weight_terms(other + c * chunk)
        copy = remote(
            part.at[pl.ds(other + c * chunk, chunk)],
            from_core.at[pl.ds(c * chunk, chunk)],
            c_send.at[c],
            c_recv.at[c],
            partner,
        )
        copy.start()
        to_core.append(copy)

    def from_sides(q):
        where = pl.ds((q + 1) * num_sent, num_sent)
        return (from_x.at[0, where], from_x.at[1, where])

    @pl.when(has_west)
    def _():
        grads_east.wait_recv()

    @pl.when(has_east)
    def _():
        grads_west.wait_recv()

    @pl.when(jnp.logical_not(has_west))
    def _():
        from_x[0] = jnp.zeros_like(from_x[0])

    @pl.when(jnp.logical_not(has_east))
    def _():
        from_x[1] = jnp.zeros_like(from_x[1])

    own_halo = [
        pltpu.make_async_copy(
            grad_ext.at[pl.ds(base + (3 + i) * num_sent, num_sent)], to_y.at[i], in_sem.at[4 + i]
        )
        for i in range(2)
    ]
    for load in own_halo:
        load.start()
    for i, q in enumerate((-1, 1)):
        own_halo[i].wait()
        left, right = from_sides(q)
        to_y[i] = to_y[i] + left[...] + right[...]
    sums_south = remote(to_y.at[0], from_y.at[1], by_send.at[0], by_recv.at[0], south)
    sums_north = remote(to_y.at[1], from_y.at[0], by_send.at[1], by_recv.at[1], north)

    @pl.when(has_south)
    def _():
        sums_south.start()

    @pl.when(has_north)
    def _():
        sums_north.start()

    for c in range(2):
        weight_terms(own + c * chunk)
    for c in range(2):
        to_core[c].wait_recv()
        part[pl.ds(own + c * chunk, chunk)] += from_core[c * chunk : (c + 1) * chunk]

    def plane_copy(d):
        p = lax.rem(here + d, n_plane)
        src = part.at[pl.ds(own, half), pl.ds(pl.multiple_of(p * piece, piece), piece)]
        return remote(src, from_plane.at[d - 1], p_send.at[d - 1], p_recv.at[d - 1], plane_device(p))

    def plane_start(d, carry):
        plane_copy(d).start()
        return carry

    lax.fori_loop(1, n_plane, plane_start, 0)

    loads[2].wait()
    group = 8 if num_blocks % 8 == 0 else num_blocks
    for first in range(0, num_blocks, group):

        def step(pair, carry):
            rhs = taps[pl.ds(2 * pair, 2)].reshape(2 * channels, channels)
            other_k = jnp.minimum(2 * pair + 1, offsets - 1)
            parts = []
            for i in range(group):
                parts.append(
                    jnp.concatenate(
                        [ext[tables[first + i, 2 * pair]], ext[tables[first + i, other_k]]], axis=1
                    )
                )
            lhs = jnp.concatenate(parts, axis=0)
            terms = jnp.dot(lhs, rhs, preferred_element_type=F32)
            total[...] += terms.reshape(group, rows, channels)
            return carry

        total[...] = jnp.zeros_like(total)
        lax.fori_loop(0, (offsets + 1) // 2, step, 0)
        for i in range(group):
            b = first + i
            out_block[b] = jnp.where(b < count, total[i], jnp.zeros((rows, channels), F32)).astype(
                BF16
            )
    out_copy = pltpu.make_async_copy(out_block, out_hbm, out_sem.at[0])
    out_copy.start()

    returned_sum = from_x[0, num_sent : 2 * num_sent] + from_x[1, num_sent : 2 * num_sent]
    returned[0:num_sent] = returned_sum

    @pl.when(has_south)
    def _():
        sums_north.wait_recv()
        returned[0:num_sent] += from_y[0]

    @pl.when(has_north)
    def _():
        sums_south.wait_recv()
        returned[0:num_sent] += from_y[1]

    loads[3].wait()
    for b in range(num_blocks):
        slot = num_sent
        for s in range(num_sent):
            slot = jnp.where(sends[0, s] == b, s, slot)
        value = own_grad[b] + returned[slot]
        grad_block[b] = jnp.where(b < count, value, jnp.zeros((rows, channels), F32)).astype(BF16)
    grad_copy = pltpu.make_async_copy(grad_block, grad_hbm, out_sem.at[1])
    grad_copy.start()

    if plane_sum.shape[0] > half:
        plane_sum[half:] = jnp.zeros((plane_sum.shape[0] - half, piece, channels), F32)
    plane_sum[0:half] = part[pl.ds(own, half), pl.ds(pl.multiple_of(here * piece, piece), piece)]

    def plane_add(d, carry):
        plane_copy(d).wait_recv()
        plane_sum[0:half] += from_plane[d - 1]
        return carry

    lax.fori_loop(1, n_plane, plane_add, 0)

    def z_copy(d):
        level = lax.rem(z + d, n_z)
        src = plane_sum.at[pl.ds(level * z_depth, z_depth)]
        return remote(src, from_z.at[d - 1], z_send.at[d - 1], z_recv.at[d - 1], z_device(level))

    def z_start(d, carry):
        z_copy(d).start()
        return carry

    lax.fori_loop(1, n_z, z_start, 0)
    mine = pl.ds(z * z_depth, z_depth)
    plane_full[mine] = plane_sum[mine]

    def z_add(d, carry):
        z_copy(d).wait_recv()
        plane_full[mine] += from_z[d - 1]
        return carry

    lax.fori_loop(1, n_z, z_add, 0)

    def gather_z_copy(d):
        level = lax.rem(z + d, n_z)
        return remote(
            plane_full.at[mine],
            plane_full.at[mine],
            gz_send.at[d - 1],
            gz_recv.at[d - 1],
            z_device(level),
        )

    def gather_z_wait(d):
        level = lax.rem(z - d + n_z, n_z)
        there = pl.ds(level * z_depth, z_depth)
        remote(
            plane_full.at[there],
            plane_full.at[there],
            gz_send.at[d - 1],
            gz_recv.at[d - 1],
            z_device(level),
        ).wait_recv()

    def gather_z_start(d, carry):
        gather_z_copy(d).start()
        return carry

    def gather_z_end(d, carry):
        gather_z_wait(d)
        return carry

    lax.fori_loop(1, n_z, gather_z_start, 0)
    lax.fori_loop(1, n_z, gather_z_end, 0)

    def full_piece(p):
        return full.at[pl.ds(own, half), pl.ds(pl.multiple_of(p * piece, piece), piece)]

    def gather_plane_copy(d):
        target = plane_device(lax.rem(here + d, n_plane))
        return remote(
            plane_full.at[pl.ds(0, half)],
            full_piece(here),
            gp_send.at[d - 1],
            gp_recv.at[d - 1],
            target,
        )

    def gather_plane_start(d, carry):
        gather_plane_copy(d).start()
        return carry

    lax.fori_loop(1, n_plane, gather_plane_start, 0)
    full[pl.ds(own, half), pl.ds(pl.multiple_of(here * piece, piece), piece)] = plane_full[0:half]

    def core_copy(d):
        p = lax.rem(here - d + n_plane, n_plane)
        return remote(full_piece(p), full_piece(p), gc_send.at[d], gc_recv.at[d], partner)

    def core_wait(d):
        p = lax.rem(here - d + n_plane, n_plane)
        where = full.at[pl.ds(other, half), pl.ds(pl.multiple_of(p * piece, piece), piece)]
        remote(where, where, gc_send.at[d], gc_recv.at[d], partner).wait_recv()

    core_copy(0).start()

    def gather_plane_end(d, carry):
        p = lax.rem(here - d + n_plane, n_plane)
        remote(
            full_piece(p), full_piece(p), gp_send.at[d - 1], gp_recv.at[d - 1], plane_device(p)
        ).wait_recv()
        core_copy(d).start()
        return carry

    lax.fori_loop(1, n_plane, gather_plane_end, 0)
    own_copy = pltpu.make_async_copy(
        full.at[pl.ds(own, half)], weight_hbm.at[pl.ds(own, half)], out_sem.at[2]
    )
    own_copy.start()

    def core_end(d, carry):
        core_wait(d)
        return carry

    lax.fori_loop(0, n_plane, core_end, 0)
    other_copy = pltpu.make_async_copy(
        full.at[pl.ds(other, half)], weight_hbm.at[pl.ds(other, half)], out_sem.at[3]
    )
    other_copy.start()

    for there, copies in (
        (has_north, [to_north, sums_north]),
        (has_south, [to_south, sums_south]),
        (has_east, [to_east[0], grads_east]),
        (has_west, [to_west[0], grads_west]),
        (jnp.logical_and(has_east, has_south), [to_east[1]]),
        (jnp.logical_and(has_east, has_north), [to_east[2]]),
        (jnp.logical_and(has_west, has_south), [to_west[1]]),
        (jnp.logical_and(has_west, has_north), [to_west[2]]),
    ):

        @pl.when(there)
        def _():
            for copy in copies:
                copy.wait_send()

    for copy in to_core:
        copy.wait_send()

    def plane_drain(d, carry):
        plane_copy(d).wait_send()
        gather_plane_copy(d).wait_send()
        core_copy(d).wait_send()
        return carry

    def z_drain(d, carry):
        z_copy(d).wait_send()
        gather_z_copy(d).wait_send()
        return carry

    core_copy(0).wait_send()
    lax.fori_loop(1, n_plane, plane_drain, 0)
    lax.fori_loop(1, n_z, z_drain, 0)
    for copy in (out_copy, grad_copy, own_copy, other_copy):
        copy.wait()


def local(sizes, features, cotangent, weights, tables, send_lists, counts):
    num_blocks = tables.shape[4]
    num_sent = send_lists.shape[3]
    offsets, channels = weights.shape[0], weights.shape[1]
    rows = features.shape[3] // num_blocks
    num_ext = num_blocks + 8 * num_sent + 1
    n_y, n_sx, n_sy = sizes
    n_plane, n_z = n_y * n_sx, n_sy // 2
    half = 2 * -(-offsets // 4)
    z_depth = -(-half // n_z)
    piece = channels // n_plane

    feats = features.reshape(num_blocks, rows, channels)
    cot = cotangent.reshape(num_blocks, rows, channels)
    table = tables.reshape(offsets, num_blocks).T
    sends = send_lists.reshape(1, num_sent)
    count = counts.reshape(1, 1)
    smem = pl.BlockSpec(memory_space=pltpu.SMEM)
    vmem = pl.BlockSpec(memory_space=pltpu.VMEM)
    anywhere = pl.BlockSpec(memory_space=pl.ANY)
    block = (rows, channels)

    outgoing, grad_ext = pl.pallas_call(
        scatter_body,
        out_shape=(
            jax.ShapeDtypeStruct((num_sent,) + block, BF16),
            jax.ShapeDtypeStruct((num_ext,) + block, F32),
        ),
        in_specs=[smem, smem, smem, vmem, vmem, vmem],
        out_specs=(vmem, vmem),
        scratch_shapes=[
            pltpu.VMEM((num_blocks,) + block, BF16),
            pltpu.VMEM((offsets, channels, channels), BF16),
        ],
        compiler_params=pltpu.CompilerParams(vmem_limit_bytes=40 << 20),
        name="scatter",
    )(table, sends, count, feats, cot, weights)

    dma = pltpu.SemaphoreType.DMA
    output, input_grad, weight_sum = pl.pallas_call(
        functools.partial(main_body, sizes),
        out_shape=(
            jax.ShapeDtypeStruct((num_blocks,) + block, BF16),
            jax.ShapeDtypeStruct((num_blocks,) + block, BF16),
            jax.ShapeDtypeStruct((2 * half, channels, channels), F32),
        ),
        in_specs=[smem, smem, smem] + [anywhere] * 5,
        out_specs=(anywhere,) * 3,
        scratch_shapes=[
            pltpu.VMEM((num_ext,) + block, BF16),
            pltpu.VMEM((num_ext, channels, rows), BF16),
            pltpu.VMEM((num_blocks,) + block, BF16),
            pltpu.VMEM((offsets + 1, channels, channels), BF16),
            pltpu.VMEM((num_blocks,) + block, F32),
            pltpu.VMEM((2, 3 * num_sent) + block, F32),
            pltpu.VMEM((2, num_sent) + block, F32),
            pltpu.VMEM((2, num_sent) + block, F32),
            pltpu.VMEM((num_sent + 1,) + block, F32),
            pltpu.VMEM((2 * half, channels, channels), F32),
            pltpu.VMEM((half, channels, channels), F32),
            pltpu.VMEM((n_plane - 1, half, piece, channels), F32),
            pltpu.VMEM((n_z * z_depth, piece, channels), F32),
            pltpu.VMEM((n_z - 1, z_depth, piece, channels), F32),
            pltpu.VMEM((n_z * z_depth, piece, channels), F32),
            pltpu.VMEM((2 * half, channels, channels), F32),
            pltpu.VMEM((8 if num_blocks % 8 == 0 else num_blocks,) + block, F32),
            pltpu.VMEM((num_blocks,) + block, BF16),
            pltpu.VMEM((num_blocks,) + block, BF16),
            dma((6,)),
            dma((4,)),
            dma((2,)),
            dma((2,)),
            dma((6,)),
            dma((6,)),
            dma((2,)),
            dma((2,)),
            dma((2,)),
            dma((2,)),
            dma((2,)),
            dma((2,)),
            dma((n_plane - 1,)),
            dma((n_plane - 1,)),
            dma((n_z - 1,)),
            dma((n_z - 1,)),
            dma((n_z - 1,)),
            dma((n_z - 1,)),
            dma((n_plane - 1,)),
            dma((n_plane - 1,)),
            dma((n_plane,)),
            dma((n_plane,)),
        ],
        compiler_params=pltpu.CompilerParams(
            collective_id=0, has_side_effects=True, vmem_limit_bytes=48 << 20
        ),
        name="main",
    )(table, sends, count, feats, cot, weights, outgoing, grad_ext)

    voxels = num_blocks * rows * n_y * n_sx * n_sy
    weight_grad = weight_sum[:offsets] * (1.0 / math.sqrt(voxels))
    return (output.reshape(features.shape), input_grad.reshape(features.shape), weight_grad)


def solution(mesh):
    sizes = tuple(mesh.shape[name] for name in ("dp", "sx", "sy"))
    return jax.shard_map(
        functools.partial(local, sizes),
        mesh=mesh,
        in_specs=(
            P("dp", "sx", "sy", None, None),
            P("dp", "sx", "sy", None, None),
            P(),
            P("dp", "sx", "sy", None, None),
            P("dp", "sx", "sy", None),
            P("dp", "sx", "sy"),
        ),
        out_specs=(P("dp", "sx", "sy", None, None), P("dp", "sx", "sy", None, None), P()),
        check_vma=False,
    )
```

time: 621 us -> 103 us (0.17)
  waiting for transfers between devices: 263 us -> 0 us
  other arithmetic: 152 us -> 1.36 us
  Pallas kernels: 0 us -> 92.1 us
  local copies, waits for them, and re-layouts: 81.9 us -> 8.37 us
  matrix products: 49.6 us -> 0 us
  starting transfers between devices: 46.6 us -> 0 us
  between operations: 15 us -> 1.36 us
  loops' own time: 7.98 us -> 0 us
    psum x1 -> x0, waiting for transfers between devices: 233 us -> none  [local(): weight_grad = lax.psum(scaled_part, ('dp', 'sx', 'sy'))]
    scatter-add x7 -> x0, other arithmetic: 138 us -> none  [the longest x6 137 us: grad_group(): accum.at[picks.reshape(-1)]]
    pallas_call x0 -> x2, Pallas kernels: none -> 92.1 us  [the longest x1 79.9 us: local(): pl.pallas_call(functools.partial(main_body, sizes), out_shape=(jax.ShapeD...]
    dot_general x18 -> x0, matrix products: 49.6 us -> none  [the longest x6 18.2 us: forward_group(): jnp.einsum('kgvc,kcd->gvd', gathered, weights, preferred_element_type=jnp...]
    ppermute x16 -> x0, starting transfers between devices: 46.5 us -> none  [the longest x12 33.5 us: shifted(): return lax.ppermute(block, axis, route)]
    ppermute x16 -> x0, waiting for transfers between devices: 30.5 us -> none  [the longest x12 17.3 us: shifted(): return lax.ppermute(block, axis, route)]
    transpose x6 -> x0, local copies, waits for them, and re-layouts: 20.1 us -> none  [grad_group(): jnp.einsum('gvd,kcd->kgvc', grad_rows, weights, preferred_element_type=jn...]
    gather x7 -> x0, local copies, waits for them, and re-layouts: 17 us -> none  [the longest x6 16.4 us: forward_group(): gathered = extended[picks]]
  transfers between devices with their start and end apart: 17 -> 0, of which waited for: 4 -> 0; matrix products, arithmetic and copies ran while one was open for 44% -> 0% of each run, Pallas kernels for 0% -> 0%
where the time goes in v1:
time: 103 us
  Pallas kernels  92.1 us (89%)
  local copies, waits for them, and re-layouts  8.37 us (8%)
  other arithmetic  1.36 us (1%)
  between operations  1.36 us (1%)
    pallas_call x1, Pallas kernels, local(): pl.pallas_call(functools.partial(main_body, sizes), out_shape=(jax.ShapeD...  79.9 us
    pallas_call x1, Pallas kernels, local(): pl.pallas_call(scatter_body, out_shape=(jax.ShapeDtypeStruct((num_sent,)...  12.2 us
    unnamed x24, local copies, waits for them, and re-layouts  8.37 us

profile of v1, /device:TPU:1, one launch (start us, length us, event | category | flops | bytes accessed | tf_op | source)
XLA Modules:
  0.0 103.2 jit_solution(1147575817549741096)
XLA Ops:
  0.6 0.0 copy-start.10
  0.6 0.0 copy-start.8
  1.3 0.0 copy-start.1
  1.3 1.2 %copy-done.1 = bf16[27,128,128]{2,1,0:T(8,128)(2,1)S(1)} copy-done((bf16[27,128,128]{2,1,0:T(8,128)(2,1)S(1)}, bf16[27,128,128]{2,1,0:T(8,128)(2,1)}, u32[]{:S(2)}) %copy-start.1) | copy-done | bytes 884760
  2.5 0.0 copy-start.3
  2.5 1.1 %copy-done.3 = bf16[1,1,1,3072,128]{4,3,2,1,0:T(8,128)(2,1)S(1)} copy-done((bf16[1,1,1,3072,128]{4,3,2,1,0:T(8,128)(2,1)S(1)}, bf16[1,1,1,3072,128]{4,3,2,1,0:T(8,128)(2,1)}, u32[]{:S(2)}) %copy-start.3) | copy-done | bytes 786456
  3.6 0.0 copy-start.5
  3.6 1.1 %copy-done.5 = bf16[1,1,1,3072,128]{4,3,2,1,0:T(8,128)(2,1)S(1)} copy-done((bf16[1,1,1,3072,128]{4,3,2,1,0:T(8,128)(2,1)S(1)}, bf16[1,1,1,3072,128]{4,3,2,1,0:T(8,128)(2,1)}, u32[]{:S(2)}) %copy-start.5) | copy-done | bytes 786456
  4.8 0.0 copy-start.7
  4.8 0.7 copy-done.7
  5.5 0.0 copy-start.9
  5.5 0.7 copy-done.9
  6.1 0.0 copy-start.2
  6.1 0.0 copy-start.4
  6.1 0.0 copy-start.6
  6.1 12.2 %scatter.1 = (bf16[4,128,128]{2,1,0:T(8,128)(2,1)S(1)}, f32[57,128,128]{2,1,0:T(8,128)S(1)}) custom-call(s32[24,27]{1,0:T(8,128)S(1)} %bitcast.17, s32[1,4]{1,0:T(1,128)S(1)} %bitcast.19, s32[1,1]{1,0:T(1,128)} %bitcast.9.counts, bf16[24,128,128]{2,1,0:T(8,128)(2,1)S(1)} %bitcast.11, bf16[24,128,128]{2,1,0:T(8,128)(2,1)S(1)} %bitcast.13, ...), custom_call_target="tpu_custom_call" | custom-call | tf_op jit(solution)/shard_map/scatter/pallas_call | solution.py:685
  18.3 0.0 copy-start
  18.3 1.8 %copy-done = f32[57,128,128]{2,1,0:T(8,128)} copy-done((f32[57,128,128]{2,1,0:T(8,128)}, f32[57,128,128]{2,1,0:T(8,128)S(1)}, u32[]{:S(2)}) %copy-start) | copy-done | bytes 3735576
  20.1 0.0 copy-done.10
  20.1 0.0 copy-done.8
  20.1 0.0 copy-done.2
  20.2 0.0 copy-done.4
  20.2 0.0 copy-done.6
  20.2 79.9 %main.1 = (bf16[24,128,128]{2,1,0:T(8,128)(2,1)S(1)}, bf16[24,128,128]{2,1,0:T(8,128)(2,1)S(1)}, f32[28,128,128]{2,1,0:T(8,128)S(1)}) custom-call(s32[24,27]{1,0:T(8,128)S(1)} %bitcast.18, s32[1,4]{1,0:T(1,128)S(1)} %bitcast.20, s32[1,1]{1,0:T(1,128)} %bitcast.10.counts, bf16[24,128,128]{2,1,0:T(8,128)(2,1)S(1)} %bitcast.12, ...), custom_call_target="tpu_custom_call" | custom-call | tf_op jit(solution)/shard_map/main/pallas_call | solution.py:702
  100.1 1.4 %slice_multiply_fusion = f32[27,128,128]{2,1,0:T(8,128)} fusion(f32[28,128,128]{2,1,0:T(8,128)S(1)} %get-tuple-element.12), kind=kLoop, calls=%fused_computation | loop fusion | flops 442368 | bytes 3538944 | tf_op jit(solution)/shard_map/mul | solution.py:761
  101.4 0.9 copy.12
  102.3 0.9 copy.13
Async XLA Ops:
  0.6 19.5 %copy-start.10 = (s32[1,1,1,4]{3,2,1,0:T(1,128)S(1)}, s32[1,1,1,4]{3,2,1,0:T(1,128)}, u32[]{:S(2)}) copy-start(s32[1,1,1,4]{3,2,1,0:T(1,128)} %param.10) | copy-start | bytes 52
  0.6 19.5 %copy-start.8 = (s32[1,1,1,27,24]{3,4,2,1,0:T(8,128)S(1)}, s32[1,1,1,27,24]{3,4,2,1,0:T(8,128)}, u32[]{:S(2)}) copy-start(s32[1,1,1,27,24]{3,4,2,1,0:T(8,128)} %param.9) | copy-start | bytes 7780
  1.3 1.2 %copy-start.1 = (bf16[27,128,128]{2,1,0:T(8,128)(2,1)S(1)}, bf16[27,128,128]{2,1,0:T(8,128)(2,1)}, u32[]{:S(2)}) copy-start(bf16[27,128,128]{2,1,0:T(8,128)(2,1)} %weights.3) | copy-start | bytes 2654212
  2.5 1.1 %copy-start.3 = (bf16[1,1,1,3072,128]{4,3,2,1,0:T(8,128)(2,1)S(1)}, bf16[1,1,1,3072,128]{4,3,2,1,0:T(8,128)(2,1)}, u32[]{:S(2)}) copy-start(bf16[1,1,1,3072,128]{4,3,2,1,0:T(8,128)(2,1)} %param.6) | copy-start | bytes 2359300
  3.6 1.1 %copy-start.5 = (bf16[1,1,1,3072,128]{4,3,2,1,0:T(8,128)(2,1)S(1)}, bf16[1,1,1,3072,128]{4,3,2,1,0:T(8,128)(2,1)}, u32[]{:S(2)}) copy-start(bf16[1,1,1,3072,128]{4,3,2,1,0:T(8,128)(2,1)} %param.7) | copy-start | bytes 2359300
  4.8 0.7 copy-start.7
  5.5 0.7 copy-start.9
  6.1 14.0 %copy-start.2 = (bf16[27,128,128]{2,1,0:T(8,128)(2,1)S(1)}, bf16[27,128,128]{2,1,0:T(8,128)(2,1)}, u32[]{:S(2)}) copy-start(bf16[27,128,128]{2,1,0:T(8,128)(2,1)} %weights.3) | copy-start | bytes 2654212
  6.1 14.0 %copy-start.4 = (bf16[1,1,1,3072,128]{4,3,2,1,0:T(8,128)(2,1)S(1)}, bf16[1,1,1,3072,128]{4,3,2,1,0:T(8,128)(2,1)}, u32[]{:S(2)}) copy-start(bf16[1,1,1,3072,128]{4,3,2,1,0:T(8,128)(2,1)} %param.6) | copy-start | bytes 2359300
  6.1 14.0 %copy-start.6 = (bf16[1,1,1,3072,128]{4,3,2,1,0:T(8,128)(2,1)S(1)}, bf16[1,1,1,3072,128]{4,3,2,1,0:T(8,128)(2,1)}, u32[]{:S(2)}) copy-start(bf16[1,1,1,3072,128]{4,3,2,1,0:T(8,128)(2,1)} %param.7) | copy-start | bytes 2359300
  18.3 1.8 %copy-start = (f32[57,128,128]{2,1,0:T(8,128)}, f32[57,128,128]{2,1,0:T(8,128)S(1)}, u32[]{:S(2)}) copy-start(f32[57,128,128]{2,1,0:T(8,128)S(1)} %get-tuple-element.9.grad_ext) | copy-start | bytes 11206660
